TPU v7x, 32 devices: a whole 2x2x4 slice. The times are simulated.
32 devices in a mesh: tok: 4 (over y, core), ch: 8 (over z, x).
Axes of the slice: x: 2, y: 2, z: 4, core: 2. Of those that a mesh axis runs over, the one named last changes fastest.
Arguments:
- tokens: bfloat16 [4096, 4096], P('tok', 'ch'), may hold values from -6 to 6
- w_in: bfloat16 [4096, 16384], P('tok', 'ch'), may hold values from -0.09375 to 0.09375
- b_in: float32 [16384], P('ch'), may hold values from -3 to 3
- dw_kernel: float32 [9, 16384], P(None, 'ch'), may hold values from -2 to 2
- dw_bias: float32 [16384], P('ch'), may hold values from -3 to 3
- w_out: bfloat16 [16384, 4096], P('ch', 'tok'), may hold values from -0.0625 to 0.0625
- b_out: float32 [4096], P('ch'), may hold values from -3 to 3
Outputs:
- mixed: bfloat16 [4096, 4096], P('tok', 'ch')
All inputs are finite; a program needn't handle non-finite values.
Results may differ from a plain program's by a relative error of at most 0.0055.
Values may be sent and summed in bfloat16 or wider, within the bound.
No kernel may reach another device: no remote copies, remote signals or barrier semaphores. Data moves between devices by JAX's collectives and lax.ppermute only.
A program may use at most 128 MiB of HBM per device.

v0:
```python
import jax
import jax.numpy as jnp
from jax import lax
from jax.sharding import PartitionSpec as P

IMAGES = 2
GRIDW = 64


def with_halo(array, sides, width):
    for axis, dim in sides:
        size, length = (lax.axis_size(axis), array.shape[dim])
        up = [(i, (i + 1) % size) for i in range(size - 1)]
        down = [(j, i) for i, j in up]
        last = lax.slice_in_dim(array, length - width, length, axis=dim)
        initial = lax.slice_in_dim(array, 0, width, axis=dim)
        before = lax.ppermute(last, axis, up)
        after = lax.ppermute(initial, axis, down)
        array = jnp.concatenate([before, array, after], axis=dim)
    return array


def fetch_rims(grid):
    return with_halo(grid, (("tok", 0),), 1)


def conv_taps(padded, taps, bias, height, width):
    conv = bias + jnp.zeros(
        (height,) + padded.shape[1:2] + (width,) + padded.shape[3:], jnp.float32
    )
    for row_off in range(3):
        for col_off in range(3):
            conv = (
                conv
                + taps[3 * row_off + col_off]
                * padded[row_off : row_off + height, :, col_off : col_off + width, :]
            )
    return conv


def pad_columns(grid):
    return jnp.pad(grid, ((0, 0), (0, 0), (1, 1), (0, 0)))


def local(tokens, w_in, b_in, dw_kernel, dw_bias, w_out, b_out):
    rows = tokens.shape[0]
    hidden = w_in.shape[1]
    w_whole = lax.all_gather(w_in, "tok", axis=0, tiled=True)
    summed = jnp.dot(
        lax.all_gather(tokens, "ch", axis=1, tiled=True),
        w_whole,
        preferred_element_type=jnp.float32,
    )
    pre = (summed + b_in).astype(jnp.bfloat16)
    height = rows // (IMAGES * GRIDW)
    grid = pre.reshape(height, IMAGES, GRIDW, hidden)
    padded = pad_columns(fetch_rims(grid).astype(jnp.float32))
    conv = conv_taps(padded, dw_kernel, dw_bias, height, GRIDW)
    act = jax.nn.gelu(conv, approximate=False).astype(jnp.bfloat16).reshape(rows, hidden)
    w_cols = lax.all_gather(w_out, "tok", axis=1, tiled=True)
    flipped = lax.psum_scatter(
        lax.dot_general(w_cols, act, (((0,), (1,)), ((), ())), preferred_element_type=jnp.float32),
        "ch",
        scatter_dimension=0,
        tiled=True,
    )
    return (flipped.T + b_out).astype(jnp.bfloat16)


def solution(mesh):
    in_specs = (
        P("tok", "ch"),
        P("tok", "ch"),
        P("ch"),
        P(None, "ch"),
        P("ch"),
        P("ch", "tok"),
        P("ch"),
    )
    out_specs = P("tok", "ch")
    return jax.shard_map(local, mesh=mesh, in_specs=in_specs, out_specs=out_specs, check_vma=False)
```

profile of v0, /device:TPU:0, one launch (start us, length us, event | category | flops | bytes accessed | tf_op | source)
XLA Modules:
  0.0 669.0 jit_solution(11230460719229125539)
XLA Ops:
  6.5 0.0 all-gather.4.cloned.1.call-start
  6.5 0.7 all-gather.4.cloned.1.call-update
  7.3 0.0 all-gather.6.cloned.1.call-start
  7.3 0.7 all-gather.6.cloned.1.call-update
  8.0 0.0 all-gather.8.cloned.1.call-start
  8.1 0.7 all-gather.8.cloned.1.call-update
  8.8 0.0 reduce-scatter.2.cloned.1.call-start
  8.8 128.3 %all-gather.4.cloned.1.call-done = bf16[1024,4096]{1,0:T(8,128)(2,1)} async-done(((bf16[1024,512]{1,0:T(8,128)(2,1)}), bf16[1024,4096]{1,0:T(8,128)(2,1)}) %all-gather.4.cloned.1.call-update) | async-done | bytes 8388624 | tf_op jit(solution)/shard_map/all_gather | solution.py:50
  137.1 105.7 %all-gather.6.cloned.1.call-done = bf16[4096,2048]{1,0:T(8,128)(2,1)} async-done(((bf16[1024,2048]{1,0:T(8,128)(2,1)}), bf16[4096,2048]{1,0:T(8,128)(2,1)}) %all-gather.6.cloned.1.call-update) | async-done | bytes 16777232 | tf_op jit(solution)/shard_map/all_gather | solution.py:48
  242.7 22.7 %add_convert_fusion = bf16[1024,2048]{1,0:T(8,128)(2,1)S(1)} fusion(bf16[1024,4096]{1,0:T(8,128)(2,1)} %all-gather.4.cloned.1.call-done, bf16[4096,2048]{1,0:T(8,128)(2,1)} %all-gather.6.cloned.1.call-done, f32[2048]{0:T(1024)S(1)} %copy-done.3), kind=kOutput, calls=%fused_computation.42 | convolution fusion | flops 17184063488 | bytes 29368320 | tf_op jit(solution)/shard_map/dot_general | solution.py:49
  265.4 0.1 fusion.26
  265.6 0.0 copy-start.1
  265.6 1.3 collective-permute-start.1
  266.9 3.1 collective-permute-start
  269.9 0.1 fusion.27
  270.0 0.0 collective-permute-done.1
  270.0 1.9 collective-permute-done
  271.9 0.8 maximum_convert_fusion
  272.7 27.4 %fusion.17 = bf16[8,2,64,2048]{3,2,1,0:T(8,128)(2,1)} fusion(f32[10,2,64,2048]{3,2,1,0:T(8,128)S(1)} %maximum_convert_fusion, f32[2048]{0:T(1024)S(1)} %bitcast.32, f32[2048]{0:T(1024)S(1)} %bitcast.33, f32[2048]{0:T(1024)S(1)} %bitcast.26, f32[2048]{0:T(1024)S(1)} %bitcast.27, f32[2048]{0:T(1024)S(1)} %bitcast.28, f32[2048]{0:T(1024)S(1)} %bitcast.29, ...), kind=kLoop, calls=%fused_computation.25 | loop fusion | flops 174063616 | bytes 39927808 | tf_op jit(solution)/shard_map/convert_element_type | solution.py:59
  300.2 55.7 %all-gather.8.cloned.1.call-done = bf16[2048,4096]{1,0:T(8,128)(2,1)} async-done(((bf16[2048,1024]{1,0:T(8,128)(2,1)}), bf16[2048,4096]{1,0:T(8,128)(2,1)}) %all-gather.8.cloned.1.call-update) | async-done | bytes 16777232 | tf_op jit(solution)/shard_map/all_gather | solution.py:60
  355.9 23.4 %convolution_bitcast_fusion = f32[4096,1024]{0,1:T(8,128)} fusion(bf16[1024,2048]{1,0:T(8,128)(2,1)} %bitcast.22, bf16[2048,4096]{1,0:T(8,128)(2,1)} %all-gather.8.cloned.1.call-done), kind=kOutput, calls=%fused_computation.7 | convolution fusion | flops 17179869184 | bytes 37748736 | tf_op jit(solution)/shard_map/dot_general | solution.py:62
  379.3 0.0 reduce-scatter.2.cloned.1.call-update
  379.3 280.3 %reduce-scatter.2.cloned.1.call-done = f32[512,1024]{0,1:T(8,128)} async-done(((f32[4096,1024]{0,1:T(8,128)}), f32[512,1024]{0,1:T(8,128)}) %reduce-scatter.2.cloned.1.call-update) | async-done | bytes 2097168 | tf_op jit(solution)/shard_map/reduce_scatter | solution.py:61
  659.6 2.8 fusion.25
  (7 shorter events, 0.0 us)
Async XLA Ops:
  6.5 236.2 %copy-start.3 = (f32[2048]{0:T(1024)S(1)}, f32[2048]{0:T(1024)}, u32[]{:S(2)}) copy-start(f32[2048]{0:T(1024)} %param.9) | copy-start | bytes 24580
  6.5 130.5 %all-gather.4.cloned.1.call-start = ((), (), s32[]{:S(2)}) async-start(), calls=%async_computation.1 | async-start | bytes 9437184 | tf_op jit(solution)/shard_map/all_gather | solution.py:50
  7.3 235.5 %all-gather.6.cloned.1.call-start = ((), (), s32[]{:S(2)}) async-start(), calls=%async_computation.2 | async-start | bytes 20971520 | tf_op jit(solution)/shard_map/all_gather | solution.py:48
  8.0 347.9 %all-gather.8.cloned.1.call-start = ((), (), s32[]{:S(2)}) async-start(), calls=%async_computation.3 | async-start | bytes 20971520 | tf_op jit(solution)/shard_map/all_gather | solution.py:60
  8.7 261.2 %copy-start = (f32[9,2048]{1,0:T(8,128)S(1)}, f32[9,2048]{1,0:T(8,128)}, u32[]{:S(2)}) copy-start(f32[9,2048]{1,0:T(8,128)} %param.10) | copy-start | bytes 221188
  8.8 650.8 %reduce-scatter.2.cloned.1.call-start = ((), (), s32[]{:S(2)}) async-start(), calls=%async_computation.4 | async-start | bytes 18874368 | tf_op jit(solution)/shard_map/reduce_scatter | solution.py:61
  265.6 7.2 %copy-start.1 = (f32[2048]{0:T(1024)S(1)}, f32[2048]{0:T(1024)}, u32[]{:S(2)}) copy-start(f32[2048]{0:T(1024)} %param.11) | copy-start | bytes 24580
  265.6 4.4 collective-permute-start.1
  266.9 5.0 collective-permute-start
  379.3 280.3 %copy-start.2 = (f32[512]{0:T(512)S(1)}, f32[512]{0:T(512)}, u32[]{:S(2)}) copy-start(f32[512]{0:T(512)} %param.13) | copy-start | bytes 6148
Sparse Core Ops, SparseCore 0:
  9.4 127.6 all-gather.3
  138.6 104.0 all-gather.5
  244.3 111.5 all-gather.7
  379.4 280.1 reduce-scatter.1
where the time goes:
time: 669 us
  waiting for transfers between devices  574 us (86%)
  matrix products  46.1 us (7%)
  other arithmetic  31.1 us (5%)
  between operations  13.2 us (2%)
    reduce_scatter x1, waiting for transfers between devices, local(): lax.psum_scatter(lax.dot_general(w_cols, act, (((0,), (1,)), ((), ())), p...  280 us
    all_gather x1, waiting for transfers between devices, local(): lax.all_gather(tokens, 'ch', axis=1, tiled=True)  128 us
    all_gather x1, waiting for transfers between devices, local(): w_whole = lax.all_gather(w_in, 'tok', axis=0, tiled=True)  106 us
    all_gather x1, waiting for transfers between devices, local(): w_cols = lax.all_gather(w_out, 'tok', axis=1, tiled=True)  55.7 us
    convert_element_type x1, other arithmetic, local(): jax.nn.gelu(conv, approximate=False).astype(jnp.bfloat16)  27.4 us
    dot_general x1, matrix products, local(): lax.dot_general(w_cols, act, (((0,), (1,)), ((), ())), preferred_element_...  23.4 us
    dot_general x1, matrix products, local(): jnp.dot(lax.all_gather(tokens, 'ch', axis=1, tiled=True), w_whole, prefer...  22.7 us
  transfers between devices with their start and end apart: 6, of which 5 were waited for; matrix products, arithmetic and copies ran while one was open for 8% of the time, Pallas kernels for 0%

commit v1 on v0

--- a/solution.py
+++ b/solution.py
@@ -5,6 +5,19 @@
 
 IMAGES = 2
 GRIDW = 64
+
+
+def collect(x, axis, dim):
+    size, index, rows = (lax.axis_size(axis), lax.axis_index(axis), x.shape[dim])
+    upward = [(i, (i + 1) % size) for i in range(size)]
+    out = jnp.zeros((*x.shape[:dim], size * rows, *x.shape[dim + 1 :]), x.dtype)
+    held = x
+    for step in range(size):
+        holder = (index - step) % size
+        out = lax.dynamic_update_slice_in_dim(out, held, holder * rows, axis=dim)
+        if step < size - 1:
+            held = lax.ppermute(held, axis, upward)
+    return out
 
 
 def with_halo(array, sides, width):
@@ -57,7 +70,7 @@
     padded = pad_columns(fetch_rims(grid).astype(jnp.float32))
     conv = conv_taps(padded, dw_kernel, dw_bias, height, GRIDW)
     act = jax.nn.gelu(conv, approximate=False).astype(jnp.bfloat16).reshape(rows, hidden)
-    w_cols = lax.all_gather(w_out, "tok", axis=1, tiled=True)
+    w_cols = collect(w_out, "tok", 1)
     flipped = lax.psum_scatter(
         lax.dot_general(w_cols, act, (((0,), (1,)), ((), ())), preferred_element_type=jnp.float32),
         "ch",

time: 669 us -> 626 us (0.936)
  waiting for transfers between devices: 574 us -> 506 us
  local copies, waits for them, and re-layouts: 0.17 us -> 24.7 us
    all_gather x1, waiting for transfers between devices: 128 us -> 31.8 us  [local(): lax.all_gather(tokens, 'ch', axis=1, tiled=True)]
    ppermute x0 -> x3, waiting for transfers between devices: none -> 82.7 us  [collect(): held = lax.ppermute(held, axis, upward)]
    all_gather x1 -> x0, waiting for transfers between devices: 55.7 us -> none  [local(): w_cols = lax.all_gather(w_out, 'tok', axis=1, tiled=True)]
    dynamic_update_slice x0 -> x4, local copies, waits for them, and re-layouts: none -> 16.5 us  [collect(): out = lax.dynamic_update_slice_in_dim(out, held, holder * rows, axis=dim)]
    broadcast_in_dim x0 -> x1, local copies, waits for them, and re-layouts: none -> 6.73 us  [collect(): out = jnp.zeros((*x.shape[:dim], size * rows, *x.shape[dim + 1:]), x.dtype)]
  transfers between devices with their start and end apart: 6 -> 8, of which waited for: 5 -> 5; matrix products, arithmetic and copies ran while one was open for 8% -> 7% of each run, Pallas kernels for 0% -> 0%
where the time goes in v1:
time: 626 us
  waiting for transfers between devices  506 us (81%)
  matrix products  46.3 us (7%)
  other arithmetic  30.1 us (5%)
  local copies, waits for them, and re-layouts  24.7 us (4%)
  between operations  13.2 us (2%)
    reduce_scatter x1, waiting for transfers between devices, local(): lax.psum_scatter(lax.dot_general(w_cols, act, (((0,), (1,)), ((), ())), p...  282 us
    all_gather x1, waiting for transfers between devices, local(): w_whole = lax.all_gather(w_in, 'tok', axis=0, tiled=True)  108 us
    ppermute x3, waiting for transfers between devices, collect(): held = lax.ppermute(held, axis, upward)  82.7 us
    all_gather x1, waiting for transfers between devices, local(): lax.all_gather(tokens, 'ch', axis=1, tiled=True)  31.8 us
    convert_element_type x1, other arithmetic, local(): jax.nn.gelu(conv, approximate=False).astype(jnp.bfloat16)  27.5 us
    dot_general x1, matrix products, local(): lax.dot_general(w_cols, act, (((0,), (1,)), ((), ())), preferred_element_...  23.6 us
    dot_general x1, matrix products, local(): jnp.dot(lax.all_gather(tokens, 'ch', axis=1, tiled=True), w_whole, prefer...  22.7 us
    dynamic_update_slice x4, local copies, waits for them, and re-layouts, collect(): out = lax.dynamic_update_slice_in_dim(out, held, holder * rows, axis=dim)  16.5 us
  transfers between devices with their start and end apart: 8, of which 5 were waited for; matrix products, arithmetic and copies ran while one was open for 7% of the time, Pallas kernels for 0%

profile of v1, /device:TPU:0, one launch (start us, length us, event | category | flops | bytes accessed | tf_op | source)
XLA Modules:
  0.0 625.8 jit_solution(17801438593898503543)
XLA Ops:
  6.5 0.7 all-gather.3.cloned.1.call-update
  7.3 0.0 all-gather.5.cloned.1.call-start
  7.3 0.7 all-gather.5.cloned.1.call-update
  8.0 0.0 reduce-scatter.2.cloned.1.call-start
  8.1 0.5 collective-permute-start
  8.6 48.4 %collective-permute-done = bf16[2048,1024]{1,0:T(8,128)(2,1)} collective-permute-done((bf16[2048,1024]{1,0:T(8,128)(2,1)}, bf16[2048,1024]{1,0:T(8,128)(2,1)}, u32[]{:S(2)}, u32[]{:S(2)}) %collective-permute-start) | collective-permute-done | bytes 4194336 | tf_op jit(solution)/shard_map/ppermute | solution.py:19
  57.1 6.7 %broadcast_in_dim.2 = bf16[2048,4096]{1,0:T(8,128)(2,1)} broadcast(bf16[]{:T(256)} %constant.40.clone.1), dimensions={} | broadcast | bytes 16777218 | tf_op jit(solution)/shard_map/broadcast_in_dim | solution.py:13
  63.8 2.4 constant_dynamic-update-slice_fusion.3
  66.2 4.8 constant_dynamic-update-slice_fusion.2
  71.0 34.3 %collective-permute-done.1 = bf16[2048,1024]{1,0:T(8,128)(2,1)} collective-permute-done((bf16[2048,1024]{1,0:T(8,128)(2,1)}, bf16[2048,1024]{1,0:T(8,128)(2,1)}, u32[]{:S(2)}, u32[]{:S(2)}) %collective-permute-start.1) | collective-permute-done | bytes 4194336 | tf_op jit(solution)/shard_map/ppermute | solution.py:19
  105.3 31.8 %all-gather.3.cloned.1.call-done = bf16[1024,4096]{1,0:T(8,128)(2,1)} async-done(((bf16[1024,512]{1,0:T(8,128)(2,1)}), bf16[1024,4096]{1,0:T(8,128)(2,1)}) %all-gather.3.cloned.1.call-update) | async-done | bytes 8388624 | tf_op jit(solution)/shard_map/all_gather | solution.py:63
  137.1 108.4 %all-gather.5.cloned.1.call-done = bf16[4096,2048]{1,0:T(8,128)(2,1)} async-done(((bf16[1024,2048]{1,0:T(8,128)(2,1)}), bf16[4096,2048]{1,0:T(8,128)(2,1)}) %all-gather.5.cloned.1.call-update) | async-done | bytes 16777232 | tf_op jit(solution)/shard_map/all_gather | solution.py:61
  245.5 22.7 %add_convert_fusion = bf16[1024,2048]{1,0:T(8,128)(2,1)S(1)} fusion(bf16[1024,4096]{1,0:T(8,128)(2,1)} %all-gather.3.cloned.1.call-done, bf16[4096,2048]{1,0:T(8,128)(2,1)} %all-gather.5.cloned.1.call-done, f32[2048]{0:T(1024)S(1)} %copy-done.4), kind=kOutput, calls=%fused_computation.41 | convolution fusion | flops 17184063488 | bytes 29368320 | tf_op jit(solution)/shard_map/dot_general | solution.py:62
  268.2 0.1 fusion.26
  268.3 1.3 collective-permute-start.4
  269.6 3.2 collective-permute-start.3
  272.8 4.7 constant_dynamic-update-slice_fusion.1
  277.5 4.7 constant_dynamic-update-slice_fusion
  282.2 0.8 maximum_convert_fusion
  283.0 27.5 %fusion.17 = bf16[8,2,64,2048]{3,2,1,0:T(8,128)(2,1)} fusion(f32[10,2,64,2048]{3,2,1,0:T(8,128)S(1)} %maximum_convert_fusion, f32[2048]{0:T(1024)S(1)} %bitcast.30, f32[2048]{0:T(1024)S(1)} %bitcast.31, f32[2048]{0:T(1024)S(1)} %bitcast.24, f32[2048]{0:T(1024)S(1)} %bitcast.25, f32[2048]{0:T(1024)S(1)} %bitcast.26, f32[2048]{0:T(1024)S(1)} %bitcast.27, ...), kind=kLoop, calls=%fused_computation.24 | loop fusion | flops 174063616 | bytes 39927808 | tf_op jit(solution)/shard_map/convert_element_type | solution.py:72
  310.5 23.6 %fusion.28 = f32[4096,1024]{1,0:T(8,128)} fusion(bf16[2048,4096]{1,0:T(8,128)(2,1)} %constant_dynamic-update-slice_fusion, bf16[1024,2048]{1,0:T(8,128)(2,1)} %bitcast.20), kind=kOutput, calls=%fused_computation.53 | convolution fusion | flops 17179869184 | bytes 37748736 | tf_op jit(solution)/shard_map/dot_general | solution.py:75
  334.1 282.1 %reduce-scatter.2.cloned.1.call-done = f32[512,1024]{1,0:T(8,128)} async-done(((f32[4096,1024]{1,0:T(8,128)}), f32[512,1024]{1,0:T(8,128)}) %reduce-scatter.2.cloned.1.call-update) | async-done | bytes 2097168 | tf_op jit(solution)/shard_map/reduce_scatter | solution.py:74
  616.2 1.8 fusion.25
  618.0 1.3 copy.8
  (18 shorter events, 0.1 us)
Async XLA Ops:
  6.5 130.5 %all-gather.3.cloned.1.call-start = ((), (), s32[]{:S(2)}) async-start(), calls=%async_computation.1 | async-start | bytes 9437184 | tf_op jit(solution)/shard_map/all_gather | solution.py:63
  7.3 238.2 %all-gather.5.cloned.1.call-start = ((), (), s32[]{:S(2)}) async-start(), calls=%async_computation.2 | async-start | bytes 20971520 | tf_op jit(solution)/shard_map/all_gather | solution.py:61
  8.0 608.2 %reduce-scatter.2.cloned.1.call-start = ((), (), s32[]{:S(2)}) async-start(), calls=%async_computation.3 | async-start | bytes 18874368 | tf_op jit(solution)/shard_map/reduce_scatter | solution.py:74
  8.1 49.0 %collective-permute-start = (bf16[2048,1024]{1,0:T(8,128)(2,1)}, bf16[2048,1024]{1,0:T(8,128)(2,1)}, u32[]{:S(2)}, u32[]{:S(2)}) collective-permute-start(bf16[2048,1024]{1,0:T(8,128)(2,1)} %param.12), channel_id=1, source_target_pairs={{0,8},{8,16},{16,24},{24,0},{1,9},{9,17},{17,25},{25,1},{2,10},{10... | collective-permute-start | bytes 12582920 | tf_op jit(solution)/shard_map/ppermute | solution.py:19
  57.0 48.2 %collective-permute-start.1 = (bf16[2048,1024]{1,0:T(8,128)(2,1)}, bf16[2048,1024]{1,0:T(8,128)(2,1)}, u32[]{:S(2)}, u32[]{:S(2)}) collective-permute-start(bf16[2048,1024]{1,0:T(8,128)(2,1)} %collective-permute-done), channel_id=1, source_target_pairs={{0,8},{8,16},{16,24},{24,0},{1,9},{9,17},{17,25},{25,1},{2,10},{10... | collective-permute-start | bytes 12582920 | tf_op jit(solution)/shard_map/ppermute | solution.py:19
  57.0 6.7 %copy-start = (bf16[2048,1024]{1,0:T(8,128)(2,1)S(1)}, bf16[2048,1024]{1,0:T(8,128)(2,1)}, u32[]{:S(2)}) copy-start(bf16[2048,1024]{1,0:T(8,128)(2,1)} %param.12) | copy-start | bytes 12582916
  63.8 2.4 copy-start.1
  63.8 181.7 %copy-start.4 = (f32[2048]{0:T(1024)S(1)}, f32[2048]{0:T(1024)}, u32[]{:S(2)}) copy-start(f32[2048]{0:T(1024)} %param.9) | copy-start | bytes 24580
  105.3 172.2 %collective-permute-start.2 = (bf16[2048,1024]{1,0:T(8,128)(2,1)}, bf16[2048,1024]{1,0:T(8,128)(2,1)}, u32[]{:S(2)}, u32[]{:S(2)}) collective-permute-start(bf16[2048,1024]{1,0:T(8,128)(2,1)} %collective-permute-done.1), channel_id=1, source_target_pairs={{0,8},{8,16},{16,24},{24,0},{1,9},{9,17},{17,25},{25,1},{2,10},{10... | collective-permute-start | bytes 12582920 | tf_op jit(solution)/shard_map/ppermute | solution.py:19
  268.3 13.9 %collective-permute-start.4 = (bf16[1,2,64,2048]{3,2,1,0:T(8,128)(2,1)S(1)}, bf16[1,2,64,2048]{3,2,1,0:T(8,128)(2,1)S(1)}, u32[]{:S(2)}, u32[]{:S(2)}) collective-permute-start(bf16[1,2,64,2048]{3,2,1,0:T(8,128)(2,1)S(1)} %bitcast.22), channel_id=1, source_target_pairs={{8,0},{16,8},{24,16},{9,1},{17,9},{25,17},{10,2},{18,10},{26,18},{... | collective-permute-start | bytes 1572872 | tf_op jit(solution)/shard_map/ppermute | solution.py:31
  269.6 12.6 %collective-permute-start.3 = (bf16[1,2,64,2048]{3,2,1,0:T(8,128)(2,1)S(1)}, bf16[1,2,64,2048]{3,2,1,0:T(8,128)(2,1)S(1)}, u32[]{:S(2)}, u32[]{:S(2)}) collective-permute-start(bf16[1,2,64,2048]{3,2,1,0:T(8,128)(2,1)S(1)} %bitcast.21), channel_id=1, source_target_pairs={{0,8},{8,16},{16,24},{1,9},{9,17},{17,25},{2,10},{10,18},{18,26},{... | collective-permute-start | bytes 1572872 | tf_op jit(solution)/shard_map/ppermute | solution.py:30
  282.2 0.9 copy-start.2
  334.1 282.1 %copy-start.3 = (f32[512]{0:T(512)S(1)}, f32[512]{0:T(512)}, u32[]{:S(2)}) copy-start(f32[512]{0:T(512)} %param.13) | copy-start | bytes 6148
Sparse Core Ops, SparseCore 0:
  9.4 127.6 all-gather.2
  138.6 106.8 all-gather.4
  334.3 281.9 reduce-scatter.1
